TPU v7x, 512 devices: a whole 4x4x16 slice. The times are simulated.
512 devices in a mesh: group: 4 (over y), shard: 32 (over x_hi, z), tensor: 4 (over x_lo, core).
Axes of the slice: x: 4 (x_hi: 2, x_lo: 2; x = x_hi * 2 + x_lo), y: 4, z: 16, core: 2. Of those that a mesh axis runs over, the one named last changes fastest.
Arguments:
- mlp_deltas: bfloat16 [4, 3, 2560, 6400], P('group', None, 'shard', 'tensor'), may hold values from -6 to 6
- mlp_master: float32 [3, 2560, 6400], P(None, ('group', 'shard', 'tensor')), may hold values from -6 to 6
- mlp_momentum: float32 [3, 2560, 6400], P(None, ('group', 'shard', 'tensor')), may hold values from -3 to 3
- attn_deltas: bfloat16 [4, 2560, 2560], P('group', 'shard', 'tensor'), may hold values from -6 to 6
- attn_master: float32 [2560, 2560], P(('group', 'shard', 'tensor')), may hold values from -6 to 6
- attn_momentum: float32 [2560, 2560], P(('group', 'shard', 'tensor')), may hold values from -3 to 3
Outputs:
- new_mlp_master: float32 [3, 2560, 6400], P(None, ('group', 'shard', 'tensor'))
- new_mlp_momentum: float32 [3, 2560, 6400], P(None, ('group', 'shard', 'tensor'))
- mlp_weights: bfloat16 [3, 2560, 6400], P(None, 'shard', 'tensor')
- new_attn_master: float32 [2560, 2560], P(('group', 'shard', 'tensor'))
- new_attn_momentum: float32 [2560, 2560], P(('group', 'shard', 'tensor'))
- attn_weights: bfloat16 [2560, 2560], P('shard', 'tensor')
All inputs are finite; a program needn't handle non-finite values.
Results may differ from a plain program's by a relative error of at most 0.0075.
Values may be sent and summed in bfloat16 or wider, within the bound.
A program may use at most 64 MiB of HBM per device.

v0:
```python
import jax
import jax.numpy as jnp
from jax import lax
from jax.sharding import PartitionSpec as P

momentum_decay = 0.9
outer_rate = 0.7


def update(outer_grad, master, momentum):
    new_momentum = momentum_decay * momentum + outer_grad
    new_master = master - outer_rate * (outer_grad + momentum_decay * new_momentum)
    return (new_master, new_momentum)


def column_split(block, shards):
    count, row_count, col_count = block.shape
    return block.reshape(count, row_count, shards, col_count // shards)


def columns_in_order(moved, shards, tensors):
    count, outer, _, unit, width = moved.shape
    piece = width // (shards * tensors)
    viewed = moved.reshape(count, outer, unit, shards, tensors, piece).transpose(0, 1, 2, 4, 3, 5)
    return viewed.reshape(count, outer, unit, width)


def sectioned_view(owned, shards, tensors):
    count, unit, width = owned.shape
    piece = width // (shards * tensors)
    return owned.reshape(count, 1, 1, unit, tensors, shards, piece)


def local(mlp_deltas, mlp_master, mlp_momentum, attn_deltas, attn_master, attn_momentum):
    groups = lax.axis_size("group")
    shards = lax.axis_size("shard")
    tensors = lax.axis_size("tensor")
    owners = shards * tensors
    unit = mlp_master.shape[1]
    mlp_block = mlp_deltas[0]
    attn_block = attn_deltas[0][None]
    rows_all = (
        lax.all_to_all(
            column_split(mlp_block, shards), "shard", split_axis=2, concat_axis=1, tiled=True
        ),
        lax.all_to_all(
            column_split(attn_block, shards), "shard", split_axis=2, concat_axis=1, tiled=True
        ),
    )
    mlp_rows = rows_all[0].reshape(rows_all[0].shape[0], rows_all[0].shape[1], rows_all[0].shape[3])
    attn_rows = rows_all[1].reshape(
        rows_all[1].shape[0], rows_all[1].shape[1], rows_all[1].shape[3]
    )

    def group_split(part):
        count, row_count, piece = part.shape
        return part.reshape(count, groups, owners, unit, piece)

    moved = (
        lax.all_to_all(
            group_split(mlp_rows), ("shard", "tensor"), split_axis=2, concat_axis=4, tiled=True
        ),
        lax.all_to_all(
            group_split(attn_rows), ("shard", "tensor"), split_axis=2, concat_axis=4, tiled=True
        ),
    )
    mlp_moved = columns_in_order(moved[0], shards, tensors)
    attn_moved = columns_in_order(moved[1], shards, tensors)
    summed = (
        lax.psum_scatter(
            mlp_moved.astype(jnp.float32).astype(jnp.bfloat16),
            "group",
            scatter_dimension=1,
            tiled=True,
        ).astype(jnp.float32),
        lax.psum_scatter(
            attn_moved.astype(jnp.float32).astype(jnp.bfloat16),
            "group",
            scatter_dimension=1,
            tiled=True,
        ).astype(jnp.float32),
    )
    mlp_total = summed[0]
    attn_total = summed[1]
    mlp_grad = mlp_total.reshape(mlp_master.shape) / groups
    attn_grad = attn_total.reshape(attn_master.shape) / groups
    new_mlp_master, new_mlp_momentum = update(mlp_grad, mlp_master, mlp_momentum)
    new_attn_master, new_attn_momentum = update(attn_grad, attn_master, attn_momentum)
    mlp_cast = new_mlp_master.astype(jnp.bfloat16)
    attn_cast = new_attn_master.astype(jnp.bfloat16)[None]
    spread = (
        lax.all_to_all(
            lax.all_to_all(
                sectioned_view(mlp_cast, shards, tensors),
                "shard",
                split_axis=5,
                concat_axis=1,
                tiled=True,
            ),
            "tensor",
            split_axis=4,
            concat_axis=2,
            tiled=True,
        ),
        lax.all_to_all(
            lax.all_to_all(
                sectioned_view(attn_cast, shards, tensors),
                "shard",
                split_axis=5,
                concat_axis=1,
                tiled=True,
            ),
            "tensor",
            split_axis=4,
            concat_axis=2,
            tiled=True,
        ),
    )
    mlp_spread = spread[0].reshape(mlp_cast.shape[0], owners * unit, spread[0].shape[-1])
    attn_spread = spread[1].reshape(1, owners * unit, spread[1].shape[-1])
    gathered = (
        lax.all_gather(mlp_spread, "group", axis=1, tiled=True),
        lax.all_gather(attn_spread, "group", axis=1, tiled=True),
    )

    def row_split(part):
        count, row_count, piece = part.shape
        return part.reshape(count, shards, row_count // shards, piece)

    back = (
        lax.all_to_all(row_split(gathered[0]), "shard", split_axis=1, concat_axis=3, tiled=True),
        lax.all_to_all(row_split(gathered[1]), "shard", split_axis=1, concat_axis=3, tiled=True),
    )
    mlp_weights = back[0].reshape(mlp_block.shape)
    attn_weights = back[1].reshape(attn_block.shape)[0]
    return (
        new_mlp_master,
        new_mlp_momentum,
        mlp_weights,
        new_attn_master,
        new_attn_momentum,
        attn_weights,
    )


def solution(mesh):
    placed = (
        P("group", None, "shard", "tensor"),
        P(None, ("group", "shard", "tensor"), None),
        P(None, ("group", "shard", "tensor"), None),
        P("group", "shard", "tensor"),
        P(("group", "shard", "tensor"), None),
        P(("group", "shard", "tensor"), None),
    )
    return jax.shard_map(
        local,
        mesh=mesh,
        in_specs=placed,
        out_specs=(
            P(None, ("group", "shard", "tensor"), None),
            P(None, ("group", "shard", "tensor"), None),
            P(None, "shard", "tensor"),
            P(("group", "shard", "tensor"), None),
            P(("group", "shard", "tensor"), None),
            P("shard", "tensor"),
        ),
        check_vma=False,
    )
```

profile of v0, /device:TPU:34, one launch (start us, length us, event | category | flops | bytes accessed | tf_op | source)
XLA Modules:
  0.0 449.5 jit_solution(16315453612850049224)
XLA Ops:
  7.2 1.1 copy.62
  8.2 0.7 reshape_broadcast_in_dim_squeeze.3
  9.0 16.9 %all-to-all-start.5 = ((bf16[1,80,32,20]{1,3,0,2:T(8,128)(2,1)}), bf16[1,80,32,20]{1,3,0,2:T(8,128)(2,1)S(1)}, u32[]{:S(2)}, u32[]{:S(2)}) async-start(bf16[1,80,32,20]{1,3,0,2:T(8,128)(2,1)} %bitcast.16), calls=%async_computation.5 | async-start | bytes 393216 | tf_op jit(solution)/shard_map/all_to_all | solution.py:46
  25.9 6.9 %reshape.67 = bf16[3,80,32,50]{3,2,1,0:T(8,128)(2,1)S(1)} reshape(bf16[1,3,80,1600]{3,2,1,0:T(8,128)(2,1)} %param.6) | data formatting | bytes 1536000 | tf_op jit(solution)/shard_map/reshape;squeeze | solution.py:18
  32.8 3.2 copy.50
  36.0 9.7 %all-to-all-done.5 = bf16[1,80,32,20]{1,3,0,2:T(8,128)(2,1)S(1)} async-done(((bf16[1,80,32,20]{1,3,0,2:T(8,128)(2,1)}), bf16[1,80,32,20]{1,3,0,2:T(8,128)(2,1)S(1)}, u32[]{:S(2)}, u32[]{:S(2)}) %all-to-all-start.5) | async-done | bytes 102432 | tf_op jit(solution)/shard_map/all_to_all | solution.py:46
  45.7 5.1 %all-to-all-start = ((bf16[3,80,32,50]{1,3,0,2:T(8,128)(2,1)}), bf16[3,80,32,50]{1,3,0,2:T(8,128)(2,1)S(1)}, u32[]{:S(2)}, u32[]{:S(2)}) async-start(bf16[3,80,32,50]{1,3,0,2:T(8,128)(2,1)} %copy.50), calls=%async_computation | async-start | bytes 2752512 | tf_op jit(solution)/shard_map/all_to_all | solution.py:43
  51.5 0.8 copy.94
  52.4 1.2 reshape.77
  53.6 65.9 %all-to-all-done = bf16[3,80,32,50]{1,3,0,2:T(8,128)(2,1)S(1)} async-done(((bf16[3,80,32,50]{1,3,0,2:T(8,128)(2,1)}), bf16[3,80,32,50]{1,3,0,2:T(8,128)(2,1)S(1)}, u32[]{:S(2)}, u32[]{:S(2)}) %all-to-all-start) | async-done | bytes 768032 | tf_op jit(solution)/shard_map/all_to_all | solution.py:43
  119.5 7.1 %all-to-all-start.6 = ((bf16[128,2,200]{2,1,0:T(2,128)(2,1)}), bf16[128,2,200]{2,1,0:T(2,128)(2,1)S(1)}, u32[]{:S(2)}, u32[]{:S(2)}) async-start(bf16[128,2,200]{2,1,0:T(2,128)(2,1)} %reshape.77), calls=%async_computation.6 | async-start | bytes 262144 | tf_op jit(solution)/shard_map/all_to_all | solution.py:63
  126.6 2.4 copy.51
  129.0 3.7 reshape_reshape.6
  132.8 3.8 copy.93
  136.6 5.5 %reshape.71 = bf16[128,2,1500]{2,1,0:T(2,128)(2,1)} reshape(bf16[128,3,5,4,50]{4,3,2,1,0:T(4,128)(2,1)} %bitcast.126) | data formatting | bytes 1536000
  142.2 16.1 %all-to-all-start.1 = ((bf16[128,2,1500]{2,1,0:T(2,128)(2,1)}), bf16[128,2,1500]{2,1,0:T(2,128)(2,1)S(1)}, u32[]{:S(2)}, u32[]{:S(2)}) async-start(bf16[128,2,1500]{2,1,0:T(2,128)(2,1)} %reshape.71), calls=%async_computation.1 | async-start | bytes 1572864 | tf_op jit(solution)/shard_map/all_to_all | solution.py:60
  158.4 0.6 reshape.78
  159.5 2.0 reshape.70
  161.8 37.4 %all-to-all-done.1 = bf16[128,2,1500]{2,1,0:T(2,128)(2,1)S(1)} async-done(((bf16[128,2,1500]{2,1,0:T(2,128)(2,1)}), bf16[128,2,1500]{2,1,0:T(2,128)(2,1)S(1)}, u32[]{:S(2)}, u32[]{:S(2)}) %all-to-all-start.1) | async-done | bytes 768032 | tf_op jit(solution)/shard_map/all_to_all | solution.py:60
  199.2 2.2 reshape.72
  202.4 5.3 %reshape.68 = bf16[3,4,5,6400]{3,0,2,1:T(4,128)(2,1)} reshape(bf16[3,4,5,4,32,50]{5,4,3,0,2,1:T(8,128)(2,1)S(1)} %copy.78) | data formatting | bytes 1536000 | tf_op jit(solution)/shard_map/reshape | solution.py:25
  207.9 1.5 fusion.4
  209.9 0.8 reshape.79
  210.7 8.3 %all-to-all-start.7 = ((bf16[32,2,200]{2,1,0:T(2,128)(2,1)}), bf16[32,2,200]{2,1,0:T(2,128)(2,1)S(1)}, u32[]{:S(2)}, u32[]{:S(2)}) async-start(bf16[32,2,200]{2,1,0:T(2,128)(2,1)} %reshape.79), calls=%async_computation.8 | async-start | bytes 65536 | tf_op jit(solution)/shard_map/all_to_all | solution.py:106
  219.0 1.3 dynamic-slice
  220.3 12.8 %all-to-all-done.7 = bf16[32,2,200]{2,1,0:T(2,128)(2,1)S(1)} async-done(((bf16[32,2,200]{2,1,0:T(2,128)(2,1)}), bf16[32,2,200]{2,1,0:T(2,128)(2,1)S(1)}, u32[]{:S(2)}, u32[]{:S(2)}) %all-to-all-start.7) | async-done | bytes 25632 | tf_op jit(solution)/shard_map/all_to_all | solution.py:106
  233.6 0.8 reshape.81
  234.3 4.8 %all-to-all-start.8 = ((bf16[4,2,1600]{2,1,0:T(2,128)(2,1)}), bf16[4,2,1600]{2,1,0:T(2,128)(2,1)S(1)}, u32[]{:S(2)}, u32[]{:S(2)}) async-start(bf16[4,2,1600]{2,1,0:T(2,128)(2,1)} %reshape.81), calls=%async_computation.9 | async-start | bytes 53248 | tf_op jit(solution)/shard_map/all_to_all | solution.py:105
  239.1 26.0 %all-reduce.3.cloned.1.call-done = bf16[3,4,5,6400]{3,0,2,1:T(4,128)(2,1)} async-done(((bf16[3,4,5,6400]{3,0,2,1:T(4,128)(2,1)}), bf16[3,4,5,6400]{3,0,2,1:T(4,128)(2,1)}) %all-reduce.3.cloned.1.call-update) | async-done | bytes 768016
  265.2 3.0 fusion.6
  268.2 1.4 reshape.58
  269.9 1.3 reshape.73
  271.2 14.3 %all-to-all-start.2 = ((bf16[32,2,1500]{2,1,0:T(2,128)(2,1)}), bf16[32,2,1500]{2,1,0:T(2,128)(2,1)S(1)}, u32[]{:S(2)}, u32[]{:S(2)}) async-start(bf16[32,2,1500]{2,1,0:T(2,128)(2,1)} %reshape.73), calls=%async_computation.2 | async-start | bytes 393216 | tf_op jit(solution)/shard_map/all_to_all | solution.py:93
  285.7 18.3 %all-to-all-done.2 = bf16[32,2,1500]{2,1,0:T(2,128)(2,1)S(1)} async-done(((bf16[32,2,1500]{2,1,0:T(2,128)(2,1)}), bf16[32,2,1500]{2,1,0:T(2,128)(2,1)S(1)}, u32[]{:S(2)}, u32[]{:S(2)}) %all-to-all-start.2) | async-done | bytes 192032 | tf_op jit(solution)/shard_map/all_to_all | solution.py:93
  303.9 0.5 reshape.74
  304.7 1.5 reshape.75
  306.2 4.8 %all-to-all-start.3 = ((bf16[4,2,12000]{2,1,0:T(2,128)(2,1)}), bf16[4,2,12000]{2,1,0:T(2,128)(2,1)S(1)}, u32[]{:S(2)}, u32[]{:S(2)}) async-start(bf16[4,2,12000]{2,1,0:T(2,128)(2,1)} %reshape.75), calls=%async_computation.3 | async-start | bytes 385024 | tf_op jit(solution)/shard_map/all_to_all | solution.py:92
  311.6 13.1 %all_gather.7 = bf16[1,2560,20]{2,1,0:T(8,128)(2,1)S(1)} all-gather(bf16[1,640,20]{2,1,0:T(8,128)(2,1)S(1)} %reshape.64), channel_id=1, replica_groups=mesh['group'=4,'shard'=32,'tensor'=4] {'group'}, dimensions={1}, use_global_device_ids=true | all-gather | bytes 128000 | tf_op jit(solution)/shard_map/all_gather | solution.py:123
  324.7 1.0 copy.73
  325.7 4.6 %all-to-all-start.9 = ((bf16[1,32,80,20]{2,3,0,1:T(8,128)(2,1)}), bf16[1,32,80,20]{2,3,0,1:T(8,128)(2,1)S(1)}, u32[]{:S(2)}, u32[]{:S(2)}) async-start(bf16[1,32,80,20]{2,3,0,1:T(8,128)(2,1)} %copy.73), calls=%async_computation.10 | async-start | bytes 393216 | tf_op jit(solution)/shard_map/all_to_all | solution.py:132
  330.3 0.9 reshape.76
  331.8 19.8 %all_gather.6 = bf16[3,2560,50]{2,1,0:T(8,128)(2,1)S(1)} all-gather(bf16[3,640,50]{2,1,0:T(8,128)(2,1)S(1)} %reshape.59), channel_id=1, replica_groups=mesh['group'=4,'shard'=32,'tensor'=4] {'group'}, dimensions={1}, use_global_device_ids=true | all-gather | bytes 960000 | tf_op jit(solution)/shard_map/all_gather | solution.py:122
  351.6 2.3 copy.60
  354.0 14.7 %all-to-all-start.4 = ((bf16[3,32,80,50]{2,3,0,1:T(8,128)(2,1)}), bf16[3,32,80,50]{2,3,0,1:T(8,128)(2,1)S(1)}, u32[]{:S(2)}, u32[]{:S(2)}) async-start(bf16[3,32,80,50]{2,3,0,1:T(8,128)(2,1)} %copy.60), calls=%async_computation.4 | async-start | bytes 2752512 | tf_op jit(solution)/shard_map/all_to_all | solution.py:131
  368.8 0.8 copy.75
  369.5 65.1 %all-to-all-done.4 = bf16[3,32,80,50]{2,3,0,1:T(8,128)(2,1)S(1)} async-done(((bf16[3,32,80,50]{2,3,0,1:T(8,128)(2,1)}), bf16[3,32,80,50]{2,3,0,1:T(8,128)(2,1)S(1)}, u32[]{:S(2)}, u32[]{:S(2)}) %all-to-all-start.4) | async-done | bytes 768032 | tf_op jit(solution)/shard_map/all_to_all | solution.py:131
  434.6 3.4 copy.81
  438.0 4.6 %reshape.69 = bf16[3,80,1600]{2,1,0:T(8,128)(2,1)} reshape(bf16[3,1,80,32,50]{4,3,2,0,1:T(8,128)(2,1)S(1)} %copy.81) | data formatting | bytes 1536000
  (40 shorter events, 5.5 us)
Async XLA Ops:
  9.0 36.7 %all-to-all-start.5 = ((bf16[1,80,32,20]{1,3,0,2:T(8,128)(2,1)}), bf16[1,80,32,20]{1,3,0,2:T(8,128)(2,1)S(1)}, u32[]{:S(2)}, u32[]{:S(2)}) async-start(bf16[1,80,32,20]{1,3,0,2:T(8,128)(2,1)} %bitcast.16), calls=%async_computation.5 | async-start | bytes 393216 | tf_op jit(solution)/shard_map/all_to_all | solution.py:46
  45.7 73.8 %all-to-all-start = ((bf16[3,80,32,50]{1,3,0,2:T(8,128)(2,1)}), bf16[3,80,32,50]{1,3,0,2:T(8,128)(2,1)S(1)}, u32[]{:S(2)}, u32[]{:S(2)}) async-start(bf16[3,80,32,50]{1,3,0,2:T(8,128)(2,1)} %copy.50), calls=%async_computation | async-start | bytes 2752512 | tf_op jit(solution)/shard_map/all_to_all | solution.py:43
  119.5 22.7 %all-to-all-start.6 = ((bf16[128,2,200]{2,1,0:T(2,128)(2,1)}), bf16[128,2,200]{2,1,0:T(2,128)(2,1)S(1)}, u32[]{:S(2)}, u32[]{:S(2)}) async-start(bf16[128,2,200]{2,1,0:T(2,128)(2,1)} %reshape.77), calls=%async_computation.6 | async-start | bytes 262144 | tf_op jit(solution)/shard_map/all_to_all | solution.py:63
  142.2 57.0 %all-to-all-start.1 = ((bf16[128,2,1500]{2,1,0:T(2,128)(2,1)}), bf16[128,2,1500]{2,1,0:T(2,128)(2,1)S(1)}, u32[]{:S(2)}, u32[]{:S(2)}) async-start(bf16[128,2,1500]{2,1,0:T(2,128)(2,1)} %reshape.71), calls=%async_computation.1 | async-start | bytes 1572864 | tf_op jit(solution)/shard_map/all_to_all | solution.py:60
  158.4 49.5 %reduce-scatter.2.cloned.1.call-start = ((), (), s32[]{:S(2)}) async-start(), calls=%async_computation.11 | async-start | bytes 204800 | tf_op jit(solution)/shard_map/reduce_scatter | solution.py:76
  161.5 103.6 %all-reduce.3.cloned.1.call-start = ((), (), s32[]{:S(2)}) async-start(), calls=%async_computation.12 | async-start | bytes 2048000
  202.4 5.4 %copy-start.2 = (f32[5,2560]{1,0:T(8,128)S(1)}, f32[5,2560]{1,0:T(8,128)}, u32[]{:S(2)}) copy-start(f32[5,2560]{1,0:T(8,128)} %param.10) | copy-start | bytes 153604
  202.4 5.4 %copy-start.3 = (f32[5,2560]{1,0:T(8,128)S(1)}, f32[5,2560]{1,0:T(8,128)}, u32[]{:S(2)}) copy-start(f32[5,2560]{1,0:T(8,128)} %param.11) | copy-start | bytes 153604
  207.8 57.4 %copy-start = (f32[3,5,6400]{2,0,1:T(4,128)S(1)}, f32[3,5,6400]{2,0,1:T(4,128)}, u32[]{:S(2)}) copy-start(f32[3,5,6400]{2,0,1:T(4,128)} %param.7) | copy-start | bytes 1152004
  207.8 57.4 %copy-start.1 = (f32[3,5,6400]{2,0,1:T(4,128)S(1)}, f32[3,5,6400]{2,0,1:T(4,128)}, u32[]{:S(2)}) copy-start(f32[3,5,6400]{2,0,1:T(4,128)} %param.8) | copy-start | bytes 1152004
  210.7 22.4 %all-to-all-start.7 = ((bf16[32,2,200]{2,1,0:T(2,128)(2,1)}), bf16[32,2,200]{2,1,0:T(2,128)(2,1)S(1)}, u32[]{:S(2)}, u32[]{:S(2)}) async-start(bf16[32,2,200]{2,1,0:T(2,128)(2,1)} %reshape.79), calls=%async_computation.8 | async-start | bytes 65536 | tf_op jit(solution)/shard_map/all_to_all | solution.py:106
  234.3 36.9 %all-to-all-start.8 = ((bf16[4,2,1600]{2,1,0:T(2,128)(2,1)}), bf16[4,2,1600]{2,1,0:T(2,128)(2,1)S(1)}, u32[]{:S(2)}, u32[]{:S(2)}) async-start(bf16[4,2,1600]{2,1,0:T(2,128)(2,1)} %reshape.81), calls=%async_computation.9 | async-start | bytes 53248 | tf_op jit(solution)/shard_map/all_to_all | solution.py:105
  271.2 32.7 %all-to-all-start.2 = ((bf16[32,2,1500]{2,1,0:T(2,128)(2,1)}), bf16[32,2,1500]{2,1,0:T(2,128)(2,1)S(1)}, u32[]{:S(2)}, u32[]{:S(2)}) async-start(bf16[32,2,1500]{2,1,0:T(2,128)(2,1)} %reshape.73), calls=%async_computation.2 | async-start | bytes 393216 | tf_op jit(solution)/shard_map/all_to_all | solution.py:93
  306.2 19.5 %all-to-all-start.3 = ((bf16[4,2,12000]{2,1,0:T(2,128)(2,1)}), bf16[4,2,12000]{2,1,0:T(2,128)(2,1)S(1)}, u32[]{:S(2)}, u32[]{:S(2)}) async-start(bf16[4,2,12000]{2,1,0:T(2,128)(2,1)} %reshape.75), calls=%async_computation.3 | async-start | bytes 385024 | tf_op jit(solution)/shard_map/all_to_all | solution.py:92
  325.7 28.3 %all-to-all-start.9 = ((bf16[1,32,80,20]{2,3,0,1:T(8,128)(2,1)}), bf16[1,32,80,20]{2,3,0,1:T(8,128)(2,1)S(1)}, u32[]{:S(2)}, u32[]{:S(2)}) async-start(bf16[1,32,80,20]{2,3,0,1:T(8,128)(2,1)} %copy.73), calls=%async_computation.10 | async-start | bytes 393216 | tf_op jit(solution)/shard_map/all_to_all | solution.py:132
  354.0 80.7 %all-to-all-start.4 = ((bf16[3,32,80,50]{2,3,0,1:T(8,128)(2,1)}), bf16[3,32,80,50]{2,3,0,1:T(8,128)(2,1)S(1)}, u32[]{:S(2)}, u32[]{:S(2)}) async-start(bf16[3,32,80,50]{2,3,0,1:T(8,128)(2,1)} %copy.60), calls=%async_computation.4 | async-start | bytes 2752512 | tf_op jit(solution)/shard_map/all_to_all | solution.py:131
Sparse Core Ops, SparseCore 0:
  162.5 29.8 reduce-scatter.1
  207.9 57.2 all-reduce.2
where the time goes:
time: 451 us; the launch traced here: 449 us
  waiting for transfers between devices  235 us (52%)
  starting transfers between devices  97.2 us (22%)
  local copies, waits for them, and re-layouts  65.1 us (14%)
  blocking collectives  32.9 us (7%)
  between operations  14.4 us (3%)
  other arithmetic  4.53 us (1%)
    all_to_all x1, waiting for transfers between devices, local(): lax.all_to_all(column_split(mlp_block, shards), 'shard', split_axis=2, co...  65.9 us
    all_to_all x1, waiting for transfers between devices, local(): lax.all_to_all(row_split(gathered[0]), 'shard', split_axis=1, concat_axis...  65.1 us
    all_to_all x1, waiting for transfers between devices, local(): lax.all_to_all(group_split(mlp_rows), ('shard', 'tensor'), split_axis=2,...  37.4 us
    unnamed x25, local copies, waits for them, and re-layouts  26.7 us
    unnamed x3, waiting for transfers between devices  26.1 us
    all_gather x1, blocking collectives, local(): lax.all_gather(mlp_spread, 'group', axis=1, tiled=True)  19.8 us
    all_to_all x1, waiting for transfers between devices, local(): lax.all_to_all(sectioned_view(mlp_cast, shards, tensors), 'shard', split_...  18.3 us
    all_to_all x1, starting transfers between devices, local(): lax.all_to_all(column_split(attn_block, shards), 'shard', split_axis=2, c...  16.9 us
  transfers between devices with their start and end apart: 12, of which 8 were waited for; matrix products, arithmetic and copies ran while one was open for 13% of the time, Pallas kernels for 0%

commit v1 on v0

v1 whole, which is shorter than its diff:
```python
import functools

import jax
import jax.numpy as jnp
from jax import lax
from jax.experimental import pallas as pl
from jax.experimental.pallas import tpu as pltpu
from jax.sharding import PartitionSpec as P

momentum_decay = 0.9
outer_rate = 0.7

LANES = 128
UNIT = 5
GROUPS = 4
TENSORS = 4
OWNERS = 16
MLP_TILES = 13
ATTN_TILES = 5
TILES = 3 * MLP_TILES + ATTN_TILES
PART = TILES // GROUPS
CHUNKS = ((0, 11),)
MESH = pl.DeviceIdType.MESH


def chunk_rows(count):
    return -(-UNIT * count // 8) * 8


def tile_place(tile):
    if tile < 3 * MLP_TILES:
        return tile // MLP_TILES, tile % MLP_TILES
    return 3, tile - 3 * MLP_TILES


def tile_width(tile):
    matrix, column = tile_place(tile)
    return 64 if matrix < 3 and column == MLP_TILES - 1 else LANES


def remote(src, dst, send_sem, recv_sem, device):
    return pltpu.make_async_remote_copy(
        src_ref=src, dst_ref=dst, send_sem=send_sem, recv_sem=recv_sem,
        device_id=device, device_id_type=MESH,
    )


def kernel(
    x_ref, master_ref, mom_ref, ax_ref, amaster_ref, amom_ref,
    new_master, new_mom, weights, new_amaster, new_amom, aweights,
    tiles, sums, total, out_tiles, *rest,
):
    count = len(CHUNKS)
    per_chunk, sems = rest[: 6 * count], rest[6 * count:]
    stage = per_chunk[0::6]
    sum_send = per_chunk[1::6]
    sum_recv = per_chunk[2::6]
    held_master = per_chunk[3::6]
    held_mom = per_chunk[4::6]
    weight_recv = per_chunk[5::6]
    (a_send, a_recv, b_send, b_recv, d_send, d_recv, e_send, e_recv, local_sem) = sems

    g = lax.axis_index("group")
    s = lax.axis_index("shard")
    t = lax.axis_index("tensor")
    my_owner = lax.rem(s, 4) * 4 + t

    def peer(step):
        return (lax.rem(g + step, GROUPS), s, t)

    def owner(k):
        return (s // 8, 4 * lax.rem(s, 8) + k // 4, lax.rem(k, 4))

    def trainer(p):
        return (p // 4, g * 8 + s // 4, lax.rem(p, 4))

    def is_me(device):
        return (device[0] == g) & (device[1] == s) & (device[2] == t)

    barrier = pltpu.get_barrier_semaphore()
    for step in range(1, GROUPS):
        pl.semaphore_signal(barrier, inc=1, device_id=peer(step), device_id_type=MESH)

    def greet(k, carry):
        for device in (owner(k), trainer(k)):
            mine = is_me(device)

            @pl.when(jnp.logical_not(mine))
            def _():
                pl.semaphore_signal(barrier, inc=1, device_id=device, device_id_type=MESH)

        return carry

    lax.fori_loop(0, OWNERS, greet, 0)

    for tile in range(TILES):
        matrix, column = tile_place(tile)
        width = tile_width(tile)
        columns = slice(LANES * column, LANES * column + width)
        block = x_ref[matrix, :, columns] if matrix < 3 else ax_ref[:, columns]
        tiles[tile, :, 0:width] = block

    own_trainer = is_me(owner(my_owner)).astype(jnp.int32)
    pl.semaphore_wait(barrier, GROUPS - 1 + 2 * (OWNERS - own_trainer))

    def a_copy(c, step):
        q0, n = CHUNKS[c]
        to = lax.rem(g + step, GROUPS)
        return remote(
            tiles.at[pl.ds(PART * to + q0, n)], sums.at[g, pl.ds(q0, n)],
            a_send.at[c, step], a_recv.at[c, g], peer(step),
        )

    def a_arrival(c, step):
        q0, n = CHUNKS[c]
        source = lax.rem(g + step, GROUPS)
        return remote(
            sums.at[source, pl.ds(q0, n)], sums.at[source, pl.ds(q0, n)],
            a_send.at[c, step], a_recv.at[c, source], peer(step),
        )

    for c in range(count):
        for step in (2, 1, 3):
            a_copy(c, step).start()

    for c, (q0, n) in enumerate(CHUNKS):
        for part in range(GROUPS):
            for q in range(n):
                tile = PART * part + q0 + q
                matrix, column = tile_place(tile)
                width = tile_width(tile)
                for piece in range(TENSORS):
                    slot = part * TENSORS + piece
                    rows = slice(UNIT * q, UNIT * q + UNIT)
                    for held, mlp, attn in (
                        (held_master[c], master_ref, amaster_ref), (held_mom[c], mom_ref, amom_ref),
                    ):
                        if matrix < 3:
                            start = 1600 * piece + LANES * column
                            held[slot, rows, 0:width] = mlp[matrix, :, start:start + width]
                        else:
                            start = 640 * piece + LANES * column
                            held[slot, rows, :] = attn[:, start:start + width]

    def b_copy(c, k):
        return remote(
            sum_send[c].at[k], sum_recv[c].at[g * TENSORS + t],
            b_send.at[c, k], b_recv.at[c, g * TENSORS + t], owner(k),
        )

    def d_copy(c, p):
        return remote(
            sum_recv[c].at[p], weight_recv[c].at[my_owner],
            d_send.at[c, p], d_recv.at[c, my_owner], trainer(p),
        )

    for c, (q0, n) in enumerate(CHUNKS):
        for step in range(1, GROUPS):
            a_arrival(c, step).wait_recv()
        sources = [lax.rem(g + step, GROUPS) for step in range(1, GROUPS)]
        for q in range(q0, q0 + n):
            value = tiles[PART * g + q].astype(jnp.float32)
            for source in sources:
                value = value + sums[source, q].astype(jnp.float32)
            total[q] = value
        for k in range(OWNERS):
            for q in range(n):
                stage[c][k, UNIT * q:UNIT * q + UNIT, :] = total[q0 + q, UNIT * k:UNIT * k + UNIT, :]

        def hand_out(k, carry):
            sum_send[c][k] = stage[c][k].astype(jnp.bfloat16)
            mine = is_me(owner(k))

            @pl.when(jnp.logical_not(mine))
            def _():
                b_copy(c, k).start()

            @pl.when(mine)
            def _():
                here = pltpu.make_async_copy(
                    sum_send[c].at[k], sum_recv[c].at[g * TENSORS + t], local_sem
                )
                here.start()
                here.wait()

            return carry

        lax.fori_loop(0, OWNERS, hand_out, 0)

    for c in range(count):

        def step_rows(p, carry):
            mine = is_me(trainer(p))

            @pl.when(jnp.logical_not(mine))
            def _():
                remote(
                    sum_recv[c].at[p], sum_recv[c].at[p], b_send.at[c, p], b_recv.at[c, p], trainer(p)
                ).wait_recv()

            grad = sum_recv[c][p].astype(jnp.float32) / GROUPS
            momentum = momentum_decay * held_mom[c][p] + grad
            master = held_master[c][p] - outer_rate * (grad + momentum_decay * momentum)
            held_mom[c][p] = momentum
            held_master[c][p] = master
            sum_recv[c][p] = master.astype(jnp.bfloat16)

            @pl.when(jnp.logical_not(mine))
            def _():
                d_copy(c, p).start()

            @pl.when(mine)
            def _():
                here = pltpu.make_async_copy(
                    sum_recv[c].at[p], weight_recv[c].at[my_owner], local_sem
                )
                here.start()
                here.wait()

            return carry

        lax.fori_loop(0, OWNERS, step_rows, 0)

    for c, (q0, n) in enumerate(CHUNKS):
        for part in range(GROUPS):
            for q in range(n):
                tile = PART * part + q0 + q
                matrix, column = tile_place(tile)
                width = tile_width(tile)
                for piece in range(TENSORS):
                    slot = part * TENSORS + piece
                    rows = slice(UNIT * q, UNIT * q + UNIT)
                    for held, mlp, attn in (
                        (held_master[c], new_master, new_amaster), (held_mom[c], new_mom, new_amom),
                    ):
                        if matrix < 3:
                            start = 1600 * piece + LANES * column
                            mlp[matrix, :, start:start + width] = held[slot, rows, 0:width]
                        else:
                            start = 640 * piece + LANES * column
                            attn[:, start:start + width] = held[slot, rows, :]

    def e_copy(c, step):
        q0, n = CHUNKS[c]
        part = out_tiles.at[pl.ds(PART * g + q0, n)]
        return remote(part, part, e_send.at[c, step], e_recv.at[c, g], peer(step))

    def e_arrival(c, step):
        q0, n = CHUNKS[c]
        source = lax.rem(g + step, GROUPS)
        part = out_tiles.at[pl.ds(PART * source + q0, n)]
        return remote(part, part, e_send.at[c, step], e_recv.at[c, source], peer(step))

    for c, (q0, n) in enumerate(CHUNKS):

        def take_in(k, carry):
            @pl.when(jnp.logical_not(is_me(owner(k))))
            def _():
                remote(
                    weight_recv[c].at[k], weight_recv[c].at[k], d_send.at[c, k], d_recv.at[c, k], owner(k)
                ).wait_recv()

            stage[c][k] = weight_recv[c][k].astype(jnp.float32)
            return carry

        lax.fori_loop(0, OWNERS, take_in, 0)
        for k in range(OWNERS):
            for q in range(n):
                total[q0 + q, UNIT * k:UNIT * k + UNIT, :] = stage[c][k, UNIT * q:UNIT * q + UNIT, :]
        for q in range(q0, q0 + n):
            out_tiles[PART * g + q] = total[q].astype(jnp.bfloat16)
        for step in (2, 1, 3):
            e_copy(c, step).start()

    for c in range(count):
        for step in range(1, GROUPS):
            e_arrival(c, step).wait_recv()
    for tile in range(TILES):
        matrix, column = tile_place(tile)
        width = tile_width(tile)
        columns = slice(LANES * column, LANES * column + width)
        if matrix < 3:
            weights[matrix, :, columns] = out_tiles[tile, :, 0:width]
        else:
            aweights[:, columns] = out_tiles[tile]

    for c in range(count):
        for step in range(1, GROUPS):
            a_copy(c, step).wait_send()
            e_copy(c, step).wait_send()

        def drain(k, carry):
            @pl.when(jnp.logical_not(is_me(owner(k))))
            def _():
                b_copy(c, k).wait_send()

            @pl.when(jnp.logical_not(is_me(trainer(k))))
            def _():
                d_copy(c, k).wait_send()

            return carry

        lax.fori_loop(0, OWNERS, drain, 0)


def local(mlp_deltas, mlp_master, mlp_momentum, attn_deltas, attn_master, attn_momentum):
    x, ax = mlp_deltas[0], attn_deltas[0]
    rows = x.shape[1]
    f32, bf16 = jnp.float32, jnp.bfloat16
    scratch = [
        pltpu.VMEM((TILES, rows, LANES), bf16),
        pltpu.VMEM((GROUPS, PART, rows, LANES), bf16),
        pltpu.VMEM((PART, rows, LANES), f32),
        pltpu.VMEM((TILES, rows, LANES), bf16),
    ]
    for _, n in CHUNKS:
        shape = (OWNERS, chunk_rows(n), LANES)
        for kind in (f32, bf16, bf16, f32, f32, bf16):
            scratch.append(pltpu.VMEM(shape, kind))
    count = len(CHUNKS)
    DMA = pltpu.SemaphoreType.DMA
    scratch += [
        DMA((count, GROUPS)), DMA((count, GROUPS)),
        DMA((count, OWNERS)), DMA((count, OWNERS)),
        DMA((count, OWNERS)), DMA((count, OWNERS)),
        DMA((count, GROUPS)), DMA((count, GROUPS)),
        DMA(()),
    ]
    shapes = [
        jax.ShapeDtypeStruct(mlp_master.shape, f32),
        jax.ShapeDtypeStruct(mlp_momentum.shape, f32),
        jax.ShapeDtypeStruct(x.shape, bf16),
        jax.ShapeDtypeStruct(attn_master.shape, f32),
        jax.ShapeDtypeStruct(attn_momentum.shape, f32),
        jax.ShapeDtypeStruct(ax.shape, bf16),
    ]
    vmem = pl.BlockSpec(memory_space=pltpu.VMEM)
    return pl.pallas_call(
        kernel,
        out_shape=shapes,
        in_specs=[vmem] * 6,
        out_specs=[vmem] * 6,
        scratch_shapes=scratch,
        compiler_params=pltpu.CompilerParams(collective_id=0, has_side_effects=True),
    )(x, mlp_master, mlp_momentum, ax, attn_master, attn_momentum)


def solution(mesh):
    owned = P(None, ("group", "shard", "tensor"), None)
    attn_owned = P(("group", "shard", "tensor"), None)
    return jax.shard_map(
        local,
        mesh=mesh,
        in_specs=(
            P("group", None, "shard", "tensor"), owned, owned,
            P("group", "shard", "tensor"), attn_owned, attn_owned,
        ),
        out_specs=(
            owned, owned, P(None, "shard", "tensor"),
            attn_owned, attn_owned, P("shard", "tensor"),
        ),
        check_vma=False,
    )
```

time: 451 us -> 115 us (0.25)
  the two profiles are of different devices: /device:TPU:34 before, /device:TPU:227 now
where the time goes in v1:
time: 115 us; the launch traced here: 114 us
  Pallas kernels  104 us (90%)
  local copies, waits for them, and re-layouts  9.72 us (8%)
    pallas_call x1, Pallas kernels, local(): pl.pallas_call(kernel, out_shape=shapes, in_specs=[vmem] * 6, out_specs=[...  104 us
    unnamed x18, local copies, waits for them, and re-layouts  6.62 us
    pallas_call x2, local copies, waits for them, and re-layouts, local(): pl.pallas_call(kernel, out_shape=shapes, in_specs=[vmem] * 6, out_specs=[...  3.1 us

profile of v1, /device:TPU:227, one launch (start us, length us, event | category | flops | bytes accessed | tf_op | source)
XLA Modules:
  0.0 114.4 jit_solution(6145093552827552985)
XLA Ops:
  0.6 0.0 copy-start.2
  0.6 2.0 %copy.12.master_ref = f32[3,5,6400]{2,1,0:T(8,128)} copy(f32[3,5,6400]{2,0,1:T(4,128)} %param.7) | data formatting | bytes 768000 | tf_op args[1]
  2.7 0.0 copy-done.2
  2.7 1.0 copy.13.mom_ref
  3.6 104.0 %shard_map.109 = (f32[3,5,6400]{2,1,0:T(8,128)}, f32[3,5,6400]{2,1,0:T(8,128)}, bf16[3,80,1600]{2,1,0:T(8,128)(2,1)}, f32[5,2560]{1,0:T(8,128)}, f32[5,2560]{1,0:T(8,128)}, /*index=5*/bf16[80,640]{1,0:T(8,128)(2,1)}) custom-call(bf16[3,80,1600]{2,1,0:T(8,128)(2,1)} %bitcast.2, f32[3,5,6400]{2,1,0:T(8,128)} %copy.12.master_ref, f32[3,5,6400]{2,1,0:T(8,128)} %copy.13.mom_ref, ...), custom_call_target="tpu_custom_call" | custom-call | tf_op jit(solution)/shard_map/pallas_call | solution.py:338
  107.7 0.0 copy-start.1
  107.7 2.1 %copy.14 = f32[3,5,6400]{2,0,1:T(4,128)} copy(f32[3,5,6400]{2,1,0:T(8,128)} %get-tuple-element.6) | data formatting | bytes 768000 | tf_op jit(solution)/shard_map/pallas_call | solution.py:338
  109.8 0.0 copy-done.1
  109.8 0.0 copy-start
  109.8 1.0 copy.15
  110.8 0.2 copy-done
  111.0 0.0 copy-start.5
  111.0 0.9 copy.20
  111.9 0.0 copy-done.5
  111.9 0.0 copy-start.4
  111.9 0.6 copy.21
  112.6 0.3 copy-done.4
  112.9 0.0 copy-start.3
  112.9 0.6 copy.22
  113.5 0.3 copy-done.3
  113.8 0.6 copy.23
Async XLA Ops:
  0.6 2.0 %copy-start.2 = (f32[3,5,6400]{2,0,1:T(4,128)S(1)}, f32[3,5,6400]{2,0,1:T(4,128)}, u32[]{:S(2)}) copy-start(f32[3,5,6400]{2,0,1:T(4,128)} %param.8) | copy-start | bytes 1152004
  107.7 2.1 %copy-start.1 = (f32[3,5,6400]{2,1,0:T(8,128)S(1)}, f32[3,5,6400]{2,1,0:T(8,128)}, u32[]{:S(2)}) copy-start(f32[3,5,6400]{2,1,0:T(8,128)} %get-tuple-element.7) | copy-start | bytes 1152004
  109.8 1.2 %copy-start = (bf16[3,80,1600]{2,1,0:T(8,128)(2,1)S(1)}, bf16[3,80,1600]{2,1,0:T(8,128)(2,1)}, u32[]{:S(2)}) copy-start(bf16[3,80,1600]{2,1,0:T(8,128)(2,1)} %get-tuple-element.20) | copy-start | bytes 2304004
  111.0 0.9 copy-start.5
  111.9 0.9 copy-start.4
  112.9 0.9 copy-start.3

commit v2 on v1

--- a/solution.py
+++ b/solution.py
@@ -19,7 +19,7 @@
 ATTN_TILES = 5
 TILES = 3 * MLP_TILES + ATTN_TILES
 PART = TILES // GROUPS
-CHUNKS = ((0, 11),)
+CHUNKS = ((0, 3), (3, 8))
 MESH = pl.DeviceIdType.MESH
 
 
@@ -51,14 +51,15 @@
     tiles, sums, total, out_tiles, *rest,
 ):
     count = len(CHUNKS)
-    per_chunk, sems = rest[: 6 * count], rest[6 * count:]
-    stage = per_chunk[0::6]
-    sum_send = per_chunk[1::6]
-    sum_recv = per_chunk[2::6]
-    held_master = per_chunk[3::6]
-    held_mom = per_chunk[4::6]
-    weight_recv = per_chunk[5::6]
-    (a_send, a_recv, b_send, b_recv, d_send, d_recv, e_send, e_recv, local_sem) = sems
+    per_chunk, sems = rest[: 7 * count], rest[7 * count:]
+    stage = per_chunk[0::7]
+    sum_send = per_chunk[1::7]
+    sum_recv = per_chunk[2::7]
+    held_master = per_chunk[3::7]
+    held_mom = per_chunk[4::7]
+    weight_recv = per_chunk[5::7]
+    relay = per_chunk[6::7]
+    (a_send, a_recv, b_send, b_recv, d_send, d_recv, r_send, r_recv, e_send, e_recv, local_sem) = sems
 
     g = lax.axis_index("group")
     s = lax.axis_index("shard")
@@ -74,24 +75,51 @@
     def trainer(p):
         return (p // 4, g * 8 + s // 4, lax.rem(p, 4))
 
+    x_hi, z = s // 16, lax.rem(s, 16)
+
+    def hub(p):
+        return (p // 4, 16 * (g // 2) + z, lax.rem(p, 4))
+
+    def hub_source(slot):
+        return (2 * x_hi + slot // 8, 16 * lax.rem(slot // 4, 2) + z, lax.rem(slot, 4))
+
+    def relay_to(w):
+        return (g, 16 * x_hi + 4 * w + z // 4, t)
+
+    def relay_source(j):
+        return (g, 16 * x_hi + 4 * lax.rem(z, 4) + j, t)
+
     def is_me(device):
         return (device[0] == g) & (device[1] == s) & (device[2] == t)
 
+    def unless_me(device, action):
+        pl.when(jnp.logical_not(is_me(device)))(action)
+
     barrier = pltpu.get_barrier_semaphore()
+
+    def greet(device):
+        pl.semaphore_signal(barrier, inc=1, device_id=device, device_id_type=MESH)
+
+    def greet_senders(k, carry):
+        unless_me(trainer(k), lambda: greet(trainer(k)))
+        unless_me(hub_source(k), lambda: greet(hub_source(k)))
+        return carry
+
+    def greet_relays(j, carry):
+        unless_me(relay_source(j), lambda: greet(relay_source(j)))
+        return carry
+
     for step in range(1, GROUPS):
-        pl.semaphore_signal(barrier, inc=1, device_id=peer(step), device_id_type=MESH)
-
-    def greet(k, carry):
-        for device in (owner(k), trainer(k)):
-            mine = is_me(device)
-
-            @pl.when(jnp.logical_not(mine))
-            def _():
-                pl.semaphore_signal(barrier, inc=1, device_id=device, device_id_type=MESH)
-
-        return carry
-
-    lax.fori_loop(0, OWNERS, greet, 0)
+        greet(peer(step))
+    lax.fori_loop(0, OWNERS, greet_senders, 0)
+    lax.fori_loop(0, 4, greet_relays, 0)
+    own_slot = 4 * (2 * lax.rem(g, 2) + x_hi) + t
+    waits = (
+        GROUPS - 1 + 2 * OWNERS + 4
+        - is_me(owner(my_owner)).astype(jnp.int32)
+        - is_me(hub(GROUPS * g + t)).astype(jnp.int32)
+        - is_me(relay_to(z // 4)).astype(jnp.int32)
+    )
 
     for tile in range(TILES):
         matrix, column = tile_place(tile)
@@ -100,8 +128,7 @@
         block = x_ref[matrix, :, columns] if matrix < 3 else ax_ref[:, columns]
         tiles[tile, :, 0:width] = block
 
-    own_trainer = is_me(owner(my_owner)).astype(jnp.int32)
-    pl.semaphore_wait(barrier, GROUPS - 1 + 2 * (OWNERS - own_trainer))
+    pl.semaphore_wait(barrier, waits)
 
     def a_copy(c, step):
         q0, n = CHUNKS[c]
@@ -150,8 +177,15 @@
 
     def d_copy(c, p):
         return remote(
-            sum_recv[c].at[p], weight_recv[c].at[my_owner],
-            d_send.at[c, p], d_recv.at[c, my_owner], trainer(p),
+            sum_recv[c].at[p], relay[c].at[own_slot],
+            d_send.at[c, p], d_recv.at[c, own_slot], hub(p),
+        )
+
+    def r_copy(c, w):
+        bundle = pl.ds(4 * lax.rem(z, 4), 4)
+        return remote(
+            relay[c].at[pl.ds(4 * w, 4)], weight_recv[c].at[bundle],
+            r_send.at[c, w], r_recv.at[c, lax.rem(z, 4)], relay_to(w),
         )
 
     for c, (q0, n) in enumerate(CHUNKS):
@@ -205,14 +239,16 @@
             held_master[c][p] = master
             sum_recv[c][p] = master.astype(jnp.bfloat16)
 
-            @pl.when(jnp.logical_not(mine))
+            to_me = is_me(hub(p))
+
+            @pl.when(jnp.logical_not(to_me))
             def _():
                 d_copy(c, p).start()
 
-            @pl.when(mine)
+            @pl.when(to_me)
             def _():
                 here = pltpu.make_async_copy(
-                    sum_recv[c].at[p], weight_recv[c].at[my_owner], local_sem
+                    sum_recv[c].at[p], relay[c].at[own_slot], local_sem
                 )
                 here.start()
                 here.wait()
@@ -220,6 +256,38 @@
             return carry
 
         lax.fori_loop(0, OWNERS, step_rows, 0)
+
+    for c in range(count):
+
+        def pass_on(w, carry):
+            for piece in range(TENSORS):
+                slot = 4 * w + piece
+
+                @pl.when(jnp.logical_not(is_me(hub_source(slot))))
+                def _():
+                    remote(
+                        relay[c].at[slot], relay[c].at[slot],
+                        d_send.at[c, slot], d_recv.at[c, slot], hub_source(slot),
+                    ).wait_recv()
+
+            mine = is_me(relay_to(w))
+
+            @pl.when(jnp.logical_not(mine))
+            def _():
+                r_copy(c, w).start()
+
+            @pl.when(mine)
+            def _():
+                here = pltpu.make_async_copy(
+                    relay[c].at[pl.ds(4 * w, 4)],
+                    weight_recv[c].at[pl.ds(4 * lax.rem(z, 4), 4)], local_sem,
+                )
+                here.start()
+                here.wait()
+
+            return carry
+
+        lax.fori_loop(0, 4, pass_on, 0)
 
     for c, (q0, n) in enumerate(CHUNKS):
         for part in range(GROUPS):
@@ -253,17 +321,20 @@
 
     for c, (q0, n) in enumerate(CHUNKS):
 
-        def take_in(k, carry):
-            @pl.when(jnp.logical_not(is_me(owner(k))))
+        def take_in(j, carry):
+            bundle = weight_recv[c].at[pl.ds(4 * j, 4)]
+
+            @pl.when(jnp.logical_not(is_me(relay_source(j))))
             def _():
                 remote(
-                    weight_recv[c].at[k], weight_recv[c].at[k], d_send.at[c, k], d_recv.at[c, k], owner(k)
+                    bundle, bundle, r_send.at[c, j], r_recv.at[c, j], relay_source(j)
                 ).wait_recv()
 
-            stage[c][k] = weight_recv[c][k].astype(jnp.float32)
-            return carry
-
-        lax.fori_loop(0, OWNERS, take_in, 0)
+            for piece in range(TENSORS):
+                stage[c][4 * j + piece] = weight_recv[c][4 * j + piece].astype(jnp.float32)
+            return carry
+
+        lax.fori_loop(0, 4, take_in, 0)
         for k in range(OWNERS):
             for q in range(n):
                 total[q0 + q, UNIT * k:UNIT * k + UNIT, :] = stage[c][k, UNIT * q:UNIT * q + UNIT, :]
@@ -294,13 +365,21 @@
             def _():
                 b_copy(c, k).wait_send()
 
-            @pl.when(jnp.logical_not(is_me(trainer(k))))
+            @pl.when(jnp.logical_not(is_me(hub(k))))
             def _():
                 d_copy(c, k).wait_send()
 
             return carry
 
+        def drain_relay(w, carry):
+            @pl.when(jnp.logical_not(is_me(relay_to(w))))
+            def _():
+                r_copy(c, w).wait_send()
+
+            return carry
+
         lax.fori_loop(0, OWNERS, drain, 0)
+        lax.fori_loop(0, 4, drain_relay, 0)
 
 
 def local(mlp_deltas, mlp_master, mlp_momentum, attn_deltas, attn_master, attn_momentum):
@@ -315,7 +394,7 @@
     ]
     for _, n in CHUNKS:
         shape = (OWNERS, chunk_rows(n), LANES)
-        for kind in (f32, bf16, bf16, f32, f32, bf16):
+        for kind in (f32, bf16, bf16, f32, f32, bf16, bf16):
             scratch.append(pltpu.VMEM(shape, kind))
     count = len(CHUNKS)
     DMA = pltpu.SemaphoreType.DMA
@@ -323,6 +402,7 @@
         DMA((count, GROUPS)), DMA((count, GROUPS)),
         DMA((count, OWNERS)), DMA((count, OWNERS)),
         DMA((count, OWNERS)), DMA((count, OWNERS)),
+        DMA((count, 4)), DMA((count, 4)),
         DMA((count, GROUPS)), DMA((count, GROUPS)),
         DMA(()),
     ]

time: 115 us -> 86.8 us (0.75)
  the two profiles are of different devices: /device:TPU:227 before, /device:TPU:65 now
where the time goes in v2:
time: 86.8 us; the launch traced here: 86.5 us
  Pallas kernels  76.1 us (88%)
  local copies, waits for them, and re-layouts  9.72 us (11%)
    pallas_call x1, Pallas kernels, local(): pl.pallas_call(kernel, out_shape=shapes, in_specs=[vmem] * 6, out_specs=[...  76.1 us
    unnamed x18, local copies, waits for them, and re-layouts  6.62 us
    pallas_call x2, local copies, waits for them, and re-layouts, local(): pl.pallas_call(kernel, out_shape=shapes, in_specs=[vmem] * 6, out_specs=[...  3.1 us

profile of v2, /device:TPU:65, one launch (start us, length us, event | category | flops | bytes accessed | tf_op | source)
XLA Modules:
  0.0 86.5 jit_solution(16938935923465229598)
XLA Ops:
  0.6 0.0 copy-start.2
  0.6 2.0 %copy.12.master_ref = f32[3,5,6400]{2,1,0:T(8,128)} copy(f32[3,5,6400]{2,0,1:T(4,128)} %param.7) | data formatting | bytes 768000 | tf_op args[1]
  2.7 0.0 copy-done.2
  2.7 1.0 %copy.13.mom_ref = f32[3,5,6400]{2,1,0:T(8,128)} copy(f32[3,5,6400]{2,0,1:T(4,128)S(1)} %copy-done.2) | data formatting | bytes 768000 | tf_op args[2]
  3.6 76.1 %shard_map.109 = (f32[3,5,6400]{2,1,0:T(8,128)}, f32[3,5,6400]{2,1,0:T(8,128)}, bf16[3,80,1600]{2,1,0:T(8,128)(2,1)}, f32[5,2560]{1,0:T(8,128)}, f32[5,2560]{1,0:T(8,128)}, /*index=5*/bf16[80,640]{1,0:T(8,128)(2,1)}) custom-call(bf16[3,80,1600]{2,1,0:T(8,128)(2,1)} %bitcast.2, f32[3,5,6400]{2,1,0:T(8,128)} %copy.12.master_ref, f32[3,5,6400]{2,1,0:T(8,128)} %copy.13.mom_ref, ...), custom_call_target="tpu_custom_call" | custom-call | tf_op jit(solution)/shard_map/pallas_call | solution.py:418
  79.7 0.0 copy-start.1
  79.8 2.1 %copy.14 = f32[3,5,6400]{2,0,1:T(4,128)} copy(f32[3,5,6400]{2,1,0:T(8,128)} %get-tuple-element.6) | data formatting | bytes 768000 | tf_op jit(solution)/shard_map/pallas_call | solution.py:418
  81.9 0.0 copy-done.1
  81.9 0.0 copy-start
  81.9 1.0 %copy.15 = f32[3,5,6400]{2,0,1:T(4,128)} copy(f32[3,5,6400]{2,1,0:T(8,128)S(1)} %copy-done.1) | data formatting | bytes 768000 | tf_op jit(solution)/shard_map/pallas_call | solution.py:418
  82.9 0.2 copy-done
  83.1 0.0 copy-start.5
  83.1 0.9 %copy.20 = bf16[3,80,1600]{2,1,0:T(8,128)(2,1)} copy(bf16[3,80,1600]{2,1,0:T(8,128)(2,1)S(1)} %copy-done) | data formatting | bytes 1536000
  83.9 0.0 copy-done.5
  84.0 0.0 copy-start.4
  84.0 0.6 copy.21
  84.6 0.3 copy-done.4
  84.9 0.0 copy-start.3
  84.9 0.6 copy.22
  85.6 0.3 copy-done.3
  85.8 0.6 copy.23
Async XLA Ops:
  0.6 2.0 %copy-start.2 = (f32[3,5,6400]{2,0,1:T(4,128)S(1)}, f32[3,5,6400]{2,0,1:T(4,128)}, u32[]{:S(2)}) copy-start(f32[3,5,6400]{2,0,1:T(4,128)} %param.8) | copy-start | bytes 1152004
  79.7 2.1 %copy-start.1 = (f32[3,5,6400]{2,1,0:T(8,128)S(1)}, f32[3,5,6400]{2,1,0:T(8,128)}, u32[]{:S(2)}) copy-start(f32[3,5,6400]{2,1,0:T(8,128)} %get-tuple-element.7) | copy-start | bytes 1152004
  81.9 1.2 %copy-start = (bf16[3,80,1600]{2,1,0:T(8,128)(2,1)S(1)}, bf16[3,80,1600]{2,1,0:T(8,128)(2,1)}, u32[]{:S(2)}) copy-start(bf16[3,80,1600]{2,1,0:T(8,128)(2,1)} %get-tuple-element.20) | copy-start | bytes 2304004
  83.1 0.9 %copy-start.5 = (f32[5,2560]{1,0:T(8,128)S(1)}, f32[5,2560]{1,0:T(8,128)}, u32[]{:S(2)}) copy-start(f32[5,2560]{1,0:T(8,128)} %get-tuple-element.21) | copy-start | bytes 153604
  84.0 0.9 %copy-start.4 = (f32[5,2560]{1,0:T(8,128)S(1)}, f32[5,2560]{1,0:T(8,128)}, u32[]{:S(2)}) copy-start(f32[5,2560]{1,0:T(8,128)} %get-tuple-element.22) | copy-start | bytes 153604
  84.9 0.9 %copy-start.3 = (bf16[80,640]{1,0:T(8,128)(2,1)S(1)}, bf16[80,640]{1,0:T(8,128)(2,1)}, u32[]{:S(2)}) copy-start(bf16[80,640]{1,0:T(8,128)(2,1)} %get-tuple-element.23) | copy-start | bytes 307204

commit v3 on v2

--- a/solution.py
+++ b/solution.py
@@ -46,10 +46,12 @@
 
 
 def kernel(
-    x_ref, master_ref, mom_ref, ax_ref, amaster_ref, amom_ref,
-    new_master, new_mom, weights, new_amaster, new_amom, aweights,
-    tiles, sums, total, out_tiles, *rest,
+    *args,
 ):
+    ins, outs, in_vmem, out_vmem, rest = args[0:6], args[6:12], args[12:18], args[18:24], args[24:]
+    x_ref, master_ref, mom_ref, ax_ref, amaster_ref, amom_ref = in_vmem
+    new_master, new_mom, weights, new_amaster, new_amom, aweights = out_vmem
+    tiles, sums, total, out_tiles, *rest = rest
     count = len(CHUNKS)
     per_chunk, sems = rest[: 7 * count], rest[7 * count:]
     stage = per_chunk[0::7]
@@ -59,7 +61,7 @@
     held_mom = per_chunk[4::7]
     weight_recv = per_chunk[5::7]
     relay = per_chunk[6::7]
-    (a_send, a_recv, b_send, b_recv, d_send, d_recv, r_send, r_recv, e_send, e_recv, local_sem) = sems
+    (a_send, a_recv, b_send, b_recv, d_send, d_recv, r_send, r_recv, e_send, e_recv, local_sem, in_sem, out_sem) = sems
 
     g = lax.axis_index("group")
     s = lax.axis_index("shard")
@@ -94,6 +96,11 @@
 
     def unless_me(device, action):
         pl.when(jnp.logical_not(is_me(device)))(action)
+
+    loads = [pltpu.make_async_copy(ins[i], in_vmem[i], in_sem.at[i]) for i in range(6)]
+    stores = [pltpu.make_async_copy(out_vmem[i], outs[i], out_sem.at[i]) for i in range(6)]
+    for i in (0, 3, 1, 2, 4, 5):
+        loads[i].start()
 
     barrier = pltpu.get_barrier_semaphore()
 
@@ -121,6 +128,8 @@
         - is_me(relay_to(z // 4)).astype(jnp.int32)
     )
 
+    loads[0].wait()
+    loads[3].wait()
     for tile in range(TILES):
         matrix, column = tile_place(tile)
         width = tile_width(tile)
@@ -150,6 +159,8 @@
         for step in (2, 1, 3):
             a_copy(c, step).start()
 
+    for i in (1, 2, 4, 5):
+        loads[i].wait()
     for c, (q0, n) in enumerate(CHUNKS):
         for part in range(GROUPS):
             for q in range(n):
@@ -164,7 +175,7 @@
                     ):
                         if matrix < 3:
                             start = 1600 * piece + LANES * column
-                            held[slot, rows, 0:width] = mlp[matrix, :, start:start + width]
+                            held[slot, rows, 0:width] = mlp[:, matrix, start:start + width]
                         else:
                             start = 640 * piece + LANES * column
                             held[slot, rows, :] = attn[:, start:start + width]
@@ -303,10 +314,13 @@
                     ):
                         if matrix < 3:
                             start = 1600 * piece + LANES * column
-                            mlp[matrix, :, start:start + width] = held[slot, rows, 0:width]
+                            mlp[:, matrix, start:start + width] = held[slot, rows, 0:width]
                         else:
                             start = 640 * piece + LANES * column
                             attn[:, start:start + width] = held[slot, rows, :]
+
+    for i in (0, 1, 3, 4):
+        stores[i].start()
 
     def e_copy(c, step):
         q0, n = CHUNKS[c]
@@ -354,6 +368,8 @@
             weights[matrix, :, columns] = out_tiles[tile, :, 0:width]
         else:
             aweights[:, columns] = out_tiles[tile]
+    for i in (2, 5):
+        stores[i].start()
 
     for c in range(count):
         for step in range(1, GROUPS):
@@ -380,13 +396,32 @@
 
         lax.fori_loop(0, OWNERS, drain, 0)
         lax.fori_loop(0, 4, drain_relay, 0)
+    for store in stores:
+        store.wait()
+
+
+def finish(*args):
+    ins, outs, held, (in_sem, out_sem) = args[0:6], args[6:12], args[12:18], args[18:20]
+    loads = [pltpu.make_async_copy(ins[i], held[i], in_sem.at[i]) for i in range(6)]
+    stores = [pltpu.make_async_copy(held[i], outs[i], out_sem.at[i]) for i in range(6)]
+    for load in loads:
+        load.start()
+    for load, store in zip(loads, stores):
+        load.wait()
+        store.start()
+    for store in stores:
+        store.wait()
 
 
 def local(mlp_deltas, mlp_master, mlp_momentum, attn_deltas, attn_master, attn_momentum):
     x, ax = mlp_deltas[0], attn_deltas[0]
+    mlp_master, mlp_momentum = (a.transpose(1, 0, 2) for a in (mlp_master, mlp_momentum))
     rows = x.shape[1]
     f32, bf16 = jnp.float32, jnp.bfloat16
-    scratch = [
+    ins = (x, mlp_master, mlp_momentum, ax, attn_master, attn_momentum)
+    outs = (mlp_master, mlp_momentum, x, attn_master, attn_momentum, ax)
+    scratch = [pltpu.VMEM(a.shape, a.dtype) for a in ins + outs]
+    scratch += [
         pltpu.VMEM((TILES, rows, LANES), bf16),
         pltpu.VMEM((GROUPS, PART, rows, LANES), bf16),
         pltpu.VMEM((PART, rows, LANES), f32),
@@ -404,25 +439,29 @@
         DMA((count, OWNERS)), DMA((count, OWNERS)),
         DMA((count, 4)), DMA((count, 4)),
         DMA((count, GROUPS)), DMA((count, GROUPS)),
-        DMA(()),
+        DMA(()), DMA((6,)), DMA((6,)),
     ]
-    shapes = [
-        jax.ShapeDtypeStruct(mlp_master.shape, f32),
-        jax.ShapeDtypeStruct(mlp_momentum.shape, f32),
-        jax.ShapeDtypeStruct(x.shape, bf16),
-        jax.ShapeDtypeStruct(attn_master.shape, f32),
-        jax.ShapeDtypeStruct(attn_momentum.shape, f32),
-        jax.ShapeDtypeStruct(ax.shape, bf16),
-    ]
-    vmem = pl.BlockSpec(memory_space=pltpu.VMEM)
-    return pl.pallas_call(
+    shapes = [jax.ShapeDtypeStruct(a.shape, a.dtype) for a in outs]
+    anywhere = [pl.BlockSpec(memory_space=pl.ANY)] * 6
+    results = pl.pallas_call(
         kernel,
         out_shape=shapes,
-        in_specs=[vmem] * 6,
-        out_specs=[vmem] * 6,
+        in_specs=anywhere,
+        out_specs=anywhere,
         scratch_shapes=scratch,
         compiler_params=pltpu.CompilerParams(collective_id=0, has_side_effects=True),
-    )(x, mlp_master, mlp_momentum, ax, attn_master, attn_momentum)
+    )(*ins)
+    master, momentum, weights, amaster, amomentum, aweights = pl.pallas_call(
+        finish,
+        out_shape=shapes,
+        in_specs=anywhere,
+        out_specs=anywhere,
+        scratch_shapes=[pltpu.VMEM(a.shape, a.dtype) for a in outs] + [DMA((6,)), DMA((6,))],
+    )(*results)
+    return (
+        master.transpose(1, 0, 2), momentum.transpose(1, 0, 2), weights,
+        amaster, amomentum, aweights,
+    )
 
 
 def solution(mesh):

time: 86.8 us -> 73.9 us (0.85)
  the two profiles are of different devices: /device:TPU:65 before, /device:TPU:70 now
where the time goes in v3:
time: 73.9 us; the launch traced here: 73.5 us
  Pallas kernels  72.9 us (99%)
    pallas_call x1, Pallas kernels, local(): pl.pallas_call(kernel, out_shape=shapes, in_specs=anywhere, out_specs=any...  70.4 us
    pallas_call x1, Pallas kernels, local(): pl.pallas_call(finish, out_shape=shapes, in_specs=anywhere, out_specs=any...  2.51 us

profile of v3, /device:TPU:70, one launch (start us, length us, event | category | flops | bytes accessed | tf_op | source)
XLA Modules:
  0.0 73.5 jit_solution(17687082391010404199)
XLA Ops:
  0.6 70.4 %shard_map.109 = (f32[5,3,6400]{2,1,0:T(4,128)}, f32[5,3,6400]{2,1,0:T(4,128)}, bf16[3,80,1600]{2,1,0:T(8,128)(2,1)}, f32[5,2560]{1,0:T(8,128)}, f32[5,2560]{1,0:T(8,128)}, /*index=5*/bf16[80,640]{1,0:T(8,128)(2,1)}) custom-call(bf16[3,80,1600]{2,1,0:T(8,128)(2,1)} %bitcast.6, f32[5,3,6400]{2,1,0:T(4,128)} %bitcast.7, f32[5,3,6400]{2,1,0:T(4,128)} %bitcast.8, ...), custom_call_target="tpu_custom_call" | custom-call | tf_op jit(solution)/shard_map/pallas_call | solution.py:446
  71.0 2.5 %shard_map.110 = (f32[5,3,6400]{2,1,0:T(4,128)}, f32[5,3,6400]{2,1,0:T(4,128)}, bf16[3,80,1600]{2,1,0:T(8,128)(2,1)}, f32[5,2560]{1,0:T(8,128)}, f32[5,2560]{1,0:T(8,128)}, /*index=5*/bf16[80,640]{1,0:T(8,128)(2,1)}) custom-call(f32[5,3,6400]{2,1,0:T(4,128)} %get-tuple-element.18.args_0_, f32[5,3,6400]{2,1,0:T(4,128)} %get-tuple-element.19.args_1_, ...), custom_call_target="tpu_custom_call" | custom-call | tf_op jit(solution)/shard_map/pallas_call | solution.py:454

commit v4 on v3

--- a/solution.py
+++ b/solution.py
@@ -19,7 +19,7 @@
 ATTN_TILES = 5
 TILES = 3 * MLP_TILES + ATTN_TILES
 PART = TILES // GROUPS
-CHUNKS = ((0, 3), (3, 8))
+CHUNKS = ((0, 3), (3, 3), (6, 5))
 MESH = pl.DeviceIdType.MESH
 
 
@@ -61,7 +61,7 @@
     held_mom = per_chunk[4::7]
     weight_recv = per_chunk[5::7]
     relay = per_chunk[6::7]
-    (a_send, a_recv, b_send, b_recv, d_send, d_recv, r_send, r_recv, e_send, e_recv, local_sem, in_sem, out_sem) = sems
+    (a_send, a_recv, b_send, b_recv, d_send, d_recv, r_send, r_recv, e_send, e_recv, local_sem, in_sem, out_sem, near) = sems
 
     g = lax.axis_index("group")
     s = lax.axis_index("shard")
@@ -103,30 +103,22 @@
         loads[i].start()
 
     barrier = pltpu.get_barrier_semaphore()
+    above = (g, 16 * x_hi + lax.rem(z + 1, 16), t)
+    below = (g, 16 * x_hi + lax.rem(z + 15, 16), t)
 
     def greet(device):
         pl.semaphore_signal(barrier, inc=1, device_id=device, device_id_type=MESH)
 
-    def greet_senders(k, carry):
-        unless_me(trainer(k), lambda: greet(trainer(k)))
+    def greet_plane(k, carry):
+        unless_me(hub(k), lambda: greet(hub(k)))
         unless_me(hub_source(k), lambda: greet(hub_source(k)))
         return carry
 
-    def greet_relays(j, carry):
-        unless_me(relay_source(j), lambda: greet(relay_source(j)))
-        return carry
-
-    for step in range(1, GROUPS):
-        greet(peer(step))
-    lax.fori_loop(0, OWNERS, greet_senders, 0)
-    lax.fori_loop(0, 4, greet_relays, 0)
+    for device in (peer(1), peer(2), peer(3), above, below):
+        greet(device)
+    lax.fori_loop(0, OWNERS, greet_plane, 0)
     own_slot = 4 * (2 * lax.rem(g, 2) + x_hi) + t
-    waits = (
-        GROUPS - 1 + 2 * OWNERS + 4
-        - is_me(owner(my_owner)).astype(jnp.int32)
-        - is_me(hub(GROUPS * g + t)).astype(jnp.int32)
-        - is_me(relay_to(z // 4)).astype(jnp.int32)
-    )
+    waits = GROUPS + 1 + 2 * OWNERS - 2 * is_me(hub(GROUPS * g + t)).astype(jnp.int32)
 
     loads[0].wait()
     loads[3].wait()
@@ -180,6 +172,15 @@
                             start = 640 * piece + LANES * column
                             held[slot, rows, :] = attn[:, start:start + width]
 
+    def meet(i, carry):
+        pl.semaphore_signal(near.at[0], inc=1, device_id=above, device_id_type=MESH)
+        pl.semaphore_signal(near.at[1], inc=1, device_id=below, device_id_type=MESH)
+        pl.semaphore_wait(near.at[0], 1)
+        pl.semaphore_wait(near.at[1], 1)
+        return carry
+
+    lax.fori_loop(0, 8, meet, 0)
+
     def b_copy(c, k):
         return remote(
             sum_send[c].at[k], sum_recv[c].at[g * TENSORS + t],
@@ -267,8 +268,6 @@
             return carry
 
         lax.fori_loop(0, OWNERS, step_rows, 0)
-
-    for c in range(count):
 
         def pass_on(w, carry):
             for piece in range(TENSORS):
@@ -439,7 +438,7 @@
         DMA((count, OWNERS)), DMA((count, OWNERS)),
         DMA((count, 4)), DMA((count, 4)),
         DMA((count, GROUPS)), DMA((count, GROUPS)),
-        DMA(()), DMA((6,)), DMA((6,)),
+        DMA(()), DMA((6,)), DMA((6,)), pltpu.SemaphoreType.REGULAR((2,)),
     ]
     shapes = [jax.ShapeDtypeStruct(a.shape, a.dtype) for a in outs]
     anywhere = [pl.BlockSpec(memory_space=pl.ANY)] * 6

time: 73.9 us -> 75.6 us (1.023)
  the two profiles are of different devices: /device:TPU:70 before, /device:TPU:97 now
where the time goes in v4:
time: 75.6 us; the launch traced here: 75.4 us
  Pallas kernels  74.8 us (99%)
    pallas_call x1, Pallas kernels, local(): pl.pallas_call(kernel, out_shape=shapes, in_specs=anywhere, out_specs=any...  72.3 us
    pallas_call x1, Pallas kernels, local(): pl.pallas_call(finish, out_shape=shapes, in_specs=anywhere, out_specs=any...  2.51 us

profile of v4, /device:TPU:97, one launch (start us, length us, event | category | flops | bytes accessed | tf_op | source)
XLA Modules:
  0.0 75.4 jit_solution(9252521681287034044)
XLA Ops:
  0.6 72.3 %shard_map.109 = (f32[5,3,6400]{2,1,0:T(4,128)}, f32[5,3,6400]{2,1,0:T(4,128)}, bf16[3,80,1600]{2,1,0:T(8,128)(2,1)}, f32[5,2560]{1,0:T(8,128)}, f32[5,2560]{1,0:T(8,128)}, /*index=5*/bf16[80,640]{1,0:T(8,128)(2,1)}) custom-call(bf16[3,80,1600]{2,1,0:T(8,128)(2,1)} %bitcast.6, f32[5,3,6400]{2,1,0:T(4,128)} %bitcast.7, f32[5,3,6400]{2,1,0:T(4,128)} %bitcast.8, ...), custom_call_target="tpu_custom_call" | custom-call | tf_op jit(solution)/shard_map/pallas_call | solution.py:445
  72.9 2.5 %shard_map.110 = (f32[5,3,6400]{2,1,0:T(4,128)}, f32[5,3,6400]{2,1,0:T(4,128)}, bf16[3,80,1600]{2,1,0:T(8,128)(2,1)}, f32[5,2560]{1,0:T(8,128)}, f32[5,2560]{1,0:T(8,128)}, /*index=5*/bf16[80,640]{1,0:T(8,128)(2,1)}) custom-call(f32[5,3,6400]{2,1,0:T(4,128)} %get-tuple-element.18.args_0_, f32[5,3,6400]{2,1,0:T(4,128)} %get-tuple-element.19.args_1_, ...), custom_call_target="tpu_custom_call" | custom-call | tf_op jit(solution)/shard_map/pallas_call | solution.py:453

commit v5 on v3

--- a/solution.py
+++ b/solution.py
@@ -19,7 +19,7 @@
 ATTN_TILES = 5
 TILES = 3 * MLP_TILES + ATTN_TILES
 PART = TILES // GROUPS
-CHUNKS = ((0, 3), (3, 8))
+CHUNKS = ((0, 3), (3, 3), (6, 5))
 MESH = pl.DeviceIdType.MESH
 
 
@@ -48,9 +48,10 @@
 def kernel(
     *args,
 ):
-    ins, outs, in_vmem, out_vmem, rest = args[0:6], args[6:12], args[12:18], args[18:24], args[24:]
+    ins, outs, in_vmem, out_vmem, rest = args[0:6], args[6:11], args[11:17], args[17:21], args[21:]
     x_ref, master_ref, mom_ref, ax_ref, amaster_ref, amom_ref = in_vmem
-    new_master, new_mom, weights, new_amaster, new_amom, aweights = out_vmem
+    new_master, new_mom, new_amaster, new_amom = out_vmem
+    landed = outs[4]
     tiles, sums, total, out_tiles, *rest = rest
     count = len(CHUNKS)
     per_chunk, sems = rest[: 7 * count], rest[7 * count:]
@@ -98,7 +99,7 @@
         pl.when(jnp.logical_not(is_me(device)))(action)
 
     loads = [pltpu.make_async_copy(ins[i], in_vmem[i], in_sem.at[i]) for i in range(6)]
-    stores = [pltpu.make_async_copy(out_vmem[i], outs[i], out_sem.at[i]) for i in range(6)]
+    stores = [pltpu.make_async_copy(out_vmem[i], outs[i], out_sem.at[i]) for i in range(4)]
     for i in (0, 3, 1, 2, 4, 5):
         loads[i].start()
 
@@ -268,8 +269,6 @@
 
         lax.fori_loop(0, OWNERS, step_rows, 0)
 
-    for c in range(count):
-
         def pass_on(w, carry):
             for piece in range(TENSORS):
                 slot = 4 * w + piece
@@ -319,18 +318,18 @@
                             start = 640 * piece + LANES * column
                             attn[:, start:start + width] = held[slot, rows, :]
 
-    for i in (0, 1, 3, 4):
-        stores[i].start()
+    for store in stores:
+        store.start()
 
     def e_copy(c, step):
         q0, n = CHUNKS[c]
-        part = out_tiles.at[pl.ds(PART * g + q0, n)]
-        return remote(part, part, e_send.at[c, step], e_recv.at[c, g], peer(step))
+        part = pl.ds(PART * g + q0, n)
+        return remote(out_tiles.at[part], landed.at[part], e_send.at[c, step], e_recv.at[c, g], peer(step))
 
     def e_arrival(c, step):
         q0, n = CHUNKS[c]
         source = lax.rem(g + step, GROUPS)
-        part = out_tiles.at[pl.ds(PART * source + q0, n)]
+        part = landed.at[pl.ds(PART * source + q0, n)]
         return remote(part, part, e_send.at[c, step], e_recv.at[c, source], peer(step))
 
     for c, (q0, n) in enumerate(CHUNKS):
@@ -356,10 +355,52 @@
             out_tiles[PART * g + q] = total[q].astype(jnp.bfloat16)
         for step in (2, 1, 3):
             e_copy(c, step).start()
+        part = pl.ds(PART * g + q0, n)
+        stores.append(pltpu.make_async_copy(out_tiles.at[part], landed.at[part], out_sem.at[4 + c]))
+        stores[-1].start()
 
     for c in range(count):
         for step in range(1, GROUPS):
             e_arrival(c, step).wait_recv()
+
+    for c in range(count):
+        for step in range(1, GROUPS):
+            a_copy(c, step).wait_send()
+            e_copy(c, step).wait_send()
+
+        def drain(k, carry):
+            @pl.when(jnp.logical_not(is_me(owner(k))))
+            def _():
+                b_copy(c, k).wait_send()
+
+            @pl.when(jnp.logical_not(is_me(hub(k))))
+            def _():
+                d_copy(c, k).wait_send()
+
+            return carry
+
+        def drain_relay(w, carry):
+            @pl.when(jnp.logical_not(is_me(relay_to(w))))
+            def _():
+                r_copy(c, w).wait_send()
+
+            return carry
+
+        lax.fori_loop(0, OWNERS, drain, 0)
+        lax.fori_loop(0, 4, drain_relay, 0)
+    for store in stores:
+        store.wait()
+
+
+def finish(*args):
+    ins, outs, held, (weights, aweights, in_sem, out_sem) = args[0:5], args[5:11], args[11:16], args[16:20]
+    out_tiles = held[4]
+    loads = [pltpu.make_async_copy(ins[i], held[i], in_sem.at[i]) for i in range(5)]
+    results = held[0:4] + (weights, aweights)
+    stores = [pltpu.make_async_copy(results[i], outs[i], out_sem.at[i]) for i in range(6)]
+    for i in (4, 0, 1, 2, 3):
+        loads[i].start()
+    loads[4].wait()
     for tile in range(TILES):
         matrix, column = tile_place(tile)
         width = tile_width(tile)
@@ -368,47 +409,11 @@
             weights[matrix, :, columns] = out_tiles[tile, :, 0:width]
         else:
             aweights[:, columns] = out_tiles[tile]
-    for i in (2, 5):
+    stores[4].start()
+    stores[5].start()
+    for i in range(4):
+        loads[i].wait()
         stores[i].start()
-
-    for c in range(count):
-        for step in range(1, GROUPS):
-            a_copy(c, step).wait_send()
-            e_copy(c, step).wait_send()
-
-        def drain(k, carry):
-            @pl.when(jnp.logical_not(is_me(owner(k))))
-            def _():
-                b_copy(c, k).wait_send()
-
-            @pl.when(jnp.logical_not(is_me(hub(k))))
-            def _():
-                d_copy(c, k).wait_send()
-
-            return carry
-
-        def drain_relay(w, carry):
-            @pl.when(jnp.logical_not(is_me(relay_to(w))))
-            def _():
-                r_copy(c, w).wait_send()
-
-            return carry
-
-        lax.fori_loop(0, OWNERS, drain, 0)
-        lax.fori_loop(0, 4, drain_relay, 0)
-    for store in stores:
-        store.wait()
-
-
-def finish(*args):
-    ins, outs, held, (in_sem, out_sem) = args[0:6], args[6:12], args[12:18], args[18:20]
-    loads = [pltpu.make_async_copy(ins[i], held[i], in_sem.at[i]) for i in range(6)]
-    stores = [pltpu.make_async_copy(held[i], outs[i], out_sem.at[i]) for i in range(6)]
-    for load in loads:
-        load.start()
-    for load, store in zip(loads, stores):
-        load.wait()
-        store.start()
     for store in stores:
         store.wait()
 
@@ -419,8 +424,8 @@
     rows = x.shape[1]
     f32, bf16 = jnp.float32, jnp.bfloat16
     ins = (x, mlp_master, mlp_momentum, ax, attn_master, attn_momentum)
-    outs = (mlp_master, mlp_momentum, x, attn_master, attn_momentum, ax)
-    scratch = [pltpu.VMEM(a.shape, a.dtype) for a in ins + outs]
+    owned = (mlp_master, mlp_momentum, attn_master, attn_momentum)
+    scratch = [pltpu.VMEM(a.shape, a.dtype) for a in ins + owned]
     scratch += [
         pltpu.VMEM((TILES, rows, LANES), bf16),
         pltpu.VMEM((GROUPS, PART, rows, LANES), bf16),
@@ -439,24 +444,27 @@
         DMA((count, OWNERS)), DMA((count, OWNERS)),
         DMA((count, 4)), DMA((count, 4)),
         DMA((count, GROUPS)), DMA((count, GROUPS)),
-        DMA(()), DMA((6,)), DMA((6,)),
+        DMA(()), DMA((6,)), DMA((4 + count,)),
     ]
-    shapes = [jax.ShapeDtypeStruct(a.shape, a.dtype) for a in outs]
-    anywhere = [pl.BlockSpec(memory_space=pl.ANY)] * 6
+    shapes = [jax.ShapeDtypeStruct(a.shape, a.dtype) for a in owned]
+    landed = jax.ShapeDtypeStruct((TILES, rows, LANES), bf16)
+    anywhere = pl.BlockSpec(memory_space=pl.ANY)
     results = pl.pallas_call(
         kernel,
-        out_shape=shapes,
-        in_specs=anywhere,
-        out_specs=anywhere,
+        out_shape=shapes + [landed],
+        in_specs=[anywhere] * 6,
+        out_specs=[anywhere] * 5,
         scratch_shapes=scratch,
         compiler_params=pltpu.CompilerParams(collective_id=0, has_side_effects=True),
     )(*ins)
-    master, momentum, weights, amaster, amomentum, aweights = pl.pallas_call(
+    blocks = [jax.ShapeDtypeStruct(a.shape, a.dtype) for a in (x, ax)]
+    master, momentum, amaster, amomentum, weights, aweights = pl.pallas_call(
         finish,
-        out_shape=shapes,
-        in_specs=anywhere,
-        out_specs=anywhere,
-        scratch_shapes=[pltpu.VMEM(a.shape, a.dtype) for a in outs] + [DMA((6,)), DMA((6,))],
+        out_shape=shapes + blocks,
+        in_specs=[anywhere] * 5,
+        out_specs=[anywhere] * 6,
+        scratch_shapes=[pltpu.VMEM(a.shape, a.dtype) for a in shapes + [landed] + blocks]
+        + [DMA((5,)), DMA((6,))],
     )(*results)
     return (
         master.transpose(1, 0, 2), momentum.transpose(1, 0, 2), weights,

time: 73.9 us -> 72.7 us (0.984)
  Pallas kernels: 72.9 us -> 71.9 us
    pallas_call x2, Pallas kernels: 72.9 us -> 71.9 us  [the longest x1 69.2 us: local(): pl.pallas_call(kernel, out_shape=shapes + [landed], in_specs=[anywhere] *...]
where the time goes in v5:
time: 72.7 us; the launch traced here: 72.5 us
  Pallas kernels  71.9 us (99%)
    pallas_call x1, Pallas kernels, local(): pl.pallas_call(kernel, out_shape=shapes + [landed], in_specs=[anywhere] *...  69.2 us
    pallas_call x1, Pallas kernels, local(): pl.pallas_call(finish, out_shape=shapes + blocks, in_specs=[anywhere] * 5...  2.73 us

profile of v5, /device:TPU:70, one launch (start us, length us, event | category | flops | bytes accessed | tf_op | source)
XLA Modules:
  0.0 72.5 jit_solution(15923243414090078219)
XLA Ops:
  0.6 69.2 %shard_map.109 = (f32[5,3,6400]{2,1,0:T(4,128)}, f32[5,3,6400]{2,1,0:T(4,128)}, f32[5,2560]{1,0:T(8,128)}, f32[5,2560]{1,0:T(8,128)}, bf16[44,80,128]{2,1,0:T(8,128)(2,1)}) custom-call(bf16[3,80,1600]{2,1,0:T(8,128)(2,1)} %bitcast.6, f32[5,3,6400]{2,1,0:T(4,128)} %bitcast.7, f32[5,3,6400]{2,1,0:T(4,128)} %bitcast.8, bf16[80,640]{1,0:T(8,128)(2,1)} %bitcast.9, ...), custom_call_target="tpu_custom_call" | custom-call | tf_op jit(solution)/shard_map/pallas_call | solution.py:452
  69.8 2.7 %shard_map.110 = (f32[5,3,6400]{2,1,0:T(4,128)}, f32[5,3,6400]{2,1,0:T(4,128)}, f32[5,2560]{1,0:T(8,128)}, f32[5,2560]{1,0:T(8,128)}, bf16[3,80,1600]{2,1,0:T(8,128)(2,1)}, /*index=5*/bf16[80,640]{1,0:T(8,128)(2,1)}) custom-call(f32[5,3,6400]{2,1,0:T(4,128)} %get-tuple-element.17.args_0_, f32[5,3,6400]{2,1,0:T(4,128)} %get-tuple-element.18.args_1_, ...), custom_call_target="tpu_custom_call" | custom-call | tf_op jit(solution)/shard_map/pallas_call | solution.py:461
